TPU v7x, 32 devices: a whole 2x2x4 slice. The times are simulated.
32 devices in a mesh: ia: 4 (over y, core), ja: 2 (over x), ka: 4 (over z).
Axes of the slice: x: 2, y: 2, z: 4, core: 2. Of those that a mesh axis runs over, the one named last changes fastest.
Arguments:
- block_coords: int32 [4, 2, 4, 4, 3], P('ia', 'ja', 'ka'), may hold values from 0 to 3, as said below
- live_blocks: int32 [4, 2, 4], P('ia', 'ja', 'ka'), may hold values from 1 to 4, as said below
- counts: int32 [4, 2, 4, 4, 64, 4096], P('ia', 'ja', 'ka'), may hold values from 0 to 7
- factor_a: float32 [1024, 256], P(('ia', 'ja', 'ka')), may hold values from 0.3 to 9.6
- factor_b: float32 [512, 256], P(('ja', 'ka')), may hold values from 0.05 to 8
- factor_c: float32 [1024, 256], P('ka', 'ia'), may hold values from 0.05 to 8
Outputs:
- factor_new: float32 [1024, 256], P(('ia', 'ja', 'ka'))
Inputs may be any that keep to these rules, and one draw needn't show every extreme that they name: `block_coords`: a device's slots name distinct blocks; slot 0 is always live, and every mode-1 block of the slab has a live block on some device. `live_blocks`: on some device all 4 slots are live.
All inputs are finite; a program needn't handle non-finite values.
Results may differ from a plain program's by a relative error of at most 0.00061.
Values may be sent and summed in bfloat16 or wider, within the bound.
A program may use at most 64 MiB of HBM per device.

v0:
```python
import jax
import jax.numpy as jnp
from jax import lax
from jax.sharding import PartitionSpec as P

R = 256
BS = 64
RB1 = 4
RB2 = 4
RB3 = 4
SLOTS = 4


def make_panel(rows_b, rows_c, index_j, index_k):
    piece_b = lax.dynamic_slice_in_dim(rows_b, index_j * BS, BS, 0)
    piece_c = lax.dynamic_slice_in_dim(rows_c, index_k * BS, BS, 0)
    return (piece_b[:, None, :] * piece_c[None, :, :]).reshape(BS * BS, R).astype(jnp.bfloat16)


def add_block(phi, factor_low, panel, index_i, weight, block_counts):
    block_a = lax.dynamic_slice_in_dim(factor_low, index_i * BS, BS, 0)
    model = lax.dot_general(
        block_a, panel, (((1,), (1,)), ((), ())), preferred_element_type=jnp.float32
    )
    ratio = (block_counts.astype(jnp.float32) / model).astype(jnp.bfloat16)
    part = jnp.dot(ratio, panel, preferred_element_type=jnp.float32) * weight
    old = lax.dynamic_slice_in_dim(phi, index_i * BS, BS, 0)
    return lax.dynamic_update_slice_in_dim(phi, old + part, index_i * BS, 0)


def local(block_coords, live_blocks, counts, factor_a, factor_b, factor_c):
    coords = block_coords.reshape(SLOTS, 3)
    local_counts = counts.reshape(SLOTS, BS, BS * BS)
    weights = (jnp.arange(SLOTS, dtype=jnp.int32) < live_blocks.reshape(())).astype(jnp.float32)
    rows_b = lax.all_gather(factor_b, "ka", axis=0, tiled=True)
    rows_c = lax.all_gather(factor_c, "ia", axis=1, tiled=True)
    sums_b = rows_b.reshape(RB2, BS, R).sum(axis=1)
    sums_c = rows_c.reshape(RB3, BS, R).sum(axis=1)
    pick_j = (coords[:, 1:2] == jnp.arange(RB2, dtype=jnp.int32)[None, :]).astype(jnp.float32)
    pick_k = (coords[:, 2:3] == jnp.arange(RB3, dtype=jnp.int32)[None, :]).astype(jnp.float32)
    masses = jnp.dot(pick_j, sums_b, precision=lax.Precision.HIGHEST) * jnp.dot(
        pick_k, sums_c, precision=lax.Precision.HIGHEST
    )
    pick_i = (coords[:, 0:1] == jnp.arange(RB1, dtype=jnp.int32)[None, :]).astype(
        jnp.float32
    ) * weights[:, None]
    mass_part = lax.dot_general(
        pick_i, masses, (((0,), (0,)), ((), ())), precision=lax.Precision.HIGHEST
    )
    mass = lax.psum(mass_part, ("ja", "ka"))
    mass_rows = jnp.broadcast_to(mass[:, None, :], (RB1, BS, R)).reshape(RB1 * BS, R)
    owned = factor_a.shape[0]
    first_row = lax.axis_index(("ja", "ka")) * owned
    my_mass = lax.dynamic_slice_in_dim(mass_rows, first_row, owned, 0)
    empty = jnp.zeros((RB1 * BS, R), jnp.float32)

    def accumulate(factor_low):

        def step(phi, item):
            index_i, index_j, index_k, weight, block_counts = item
            panel = make_panel(rows_b, rows_c, index_j, index_k)
            return (add_block(phi, factor_low, panel, index_i, weight, block_counts), None)

        phi, _ = lax.scan(
            step, empty, (coords[:, 0], coords[:, 1], coords[:, 2], weights, local_counts)
        )
        return phi

    whole = lax.all_gather(factor_a, ("ja", "ka"), axis=0, tiled=True)
    phi = accumulate(whole.astype(jnp.bfloat16))
    totals = lax.psum(phi, ("ja", "ka"))
    updated = whole * totals / mass_rows
    phi = accumulate(updated.astype(jnp.bfloat16))
    mine = lax.psum_scatter(phi, ("ja", "ka"), scatter_dimension=0, tiled=True)
    return lax.dynamic_slice_in_dim(updated, first_row, owned, 0) * mine / my_mass


def solution(mesh):
    placed = (
        P("ia", "ja", "ka", None, None),
        P("ia", "ja", "ka"),
        P("ia", "ja", "ka", None, None, None),
        P(("ia", "ja", "ka"), None),
        P(("ja", "ka"), None),
        P("ka", "ia"),
    )
    return jax.shard_map(
        local, mesh=mesh, in_specs=placed, out_specs=P(("ia", "ja", "ka"), None), check_vma=False
    )
```

profile of v0, /device:TPU:0, one launch (start us, length us, event | category | flops | bytes accessed | tf_op | source)
XLA Modules:
  0.0 275.6 jit_solution(7233616077265290646)
XLA Ops:
  6.5 0.8 copy.14
  7.5 7.5 %all_gather.11 = f32[256,256]{0,1:T(8,128)S(1)} all-gather(f32[256,64]{0,1:T(8,128)} %param.15), channel_id=1, replica_groups=mesh['ia'=4,'ja'=2,'ka'=4] {'ia'}, dimensions={1}, use_global_device_ids=true | all-gather | bytes 327680 | tf_op jit(solution)/shard_map/all_gather | solution.py:36
  15.1 14.3 %all_gather.10 = f32[256,256]{1,0:T(8,128)S(1)} all-gather(f32[64,256]{1,0:T(8,128)} %param.14), channel_id=1, replica_groups=mesh['ia'=4,'ja'=2,'ka'=4] {'ka'}, dimensions={0}, use_global_device_ids=true | all-gather | bytes 327680 | tf_op jit(solution)/shard_map/all_gather | solution.py:35
  30.1 31.8 %all_gather.9 = f32[256,256]{1,0:T(8,128)S(1)} all-gather(f32[32,256]{1,0:T(8,128)} %param.13), channel_id=1, replica_groups=mesh['ia'=4,'ja'=2,'ka'=4] {'ja','ka'}, dimensions={0}, use_global_device_ids=true | all-gather | bytes 294912 | tf_op jit(solution)/shard_map/all_gather | solution.py:69
  62.0 34.4 %while.20 = (s32[]{:T(128)}, f32[256,256]{1,0:T(8,128)S(1)}, s32[4]{0:T(128)S(1)}, s32[4,64,4096]{2,1,0:T(8,128)}, bf16[256,256]{1,0:T(8,128)(2,1)S(1)}, /*index...) while((s32[]{:T(128)}, f32[256,256]{1,0:T(8,128)S(1)}, ...), condition=%wide.region_1.0_spmd, body=%wide.region_0.0_spmd.sunk | while | flops 271351808 | bytes 7899463 | solution.py:64
  64.7 0.7 multiply_convert_fusion.4
  65.4 0.7 dynamic_slice.107
  67.5 3.1 %fusion.52 = f32[256,256]{1,0:T(8,128)S(1)} fusion(f32[256,256]{1,0:T(8,128)S(1)} %get-tuple-element.345, s32[]{:T(128)S(6)} %select_n.33, bf16[4096,256]{1,0:T(8,128)(2,1)S(1)} %bitcast.70, s32[4,64,4096]{2,1,0:T(8,128)} %get-tuple-element.361, s32[]{:T(128)} %get-tuple-element.344, f32[]{:T(128)} %bitcast.60, ...), kind=kOutput, calls=%fused_computation.6.clone.1 | convolution fusion | flops 269254656 | bytes 5408768 | tf_op jit(solution)/shard_map/while/body/eval_jaxpr/dot_general | solution.py:26
  73.3 0.7 multiply_convert_fusion.4
  74.0 0.7 dynamic_slice.107
  76.1 3.1 %fusion.52 = f32[256,256]{1,0:T(8,128)S(1)} fusion(f32[256,256]{1,0:T(8,128)S(1)} %get-tuple-element.345, s32[]{:T(128)S(6)} %select_n.33, bf16[4096,256]{1,0:T(8,128)(2,1)S(1)} %bitcast.70, s32[4,64,4096]{2,1,0:T(8,128)} %get-tuple-element.361, s32[]{:T(128)} %get-tuple-element.344, f32[]{:T(128)} %bitcast.60, ...), kind=kOutput, calls=%fused_computation.6.clone.1 | convolution fusion | flops 269254656 | bytes 5408768 | tf_op jit(solution)/shard_map/while/body/eval_jaxpr/dot_general | solution.py:26
  81.9 0.7 multiply_convert_fusion.4
  82.6 0.7 dynamic_slice.107
  84.7 3.1 %fusion.52 = f32[256,256]{1,0:T(8,128)S(1)} fusion(f32[256,256]{1,0:T(8,128)S(1)} %get-tuple-element.345, s32[]{:T(128)S(6)} %select_n.33, bf16[4096,256]{1,0:T(8,128)(2,1)S(1)} %bitcast.70, s32[4,64,4096]{2,1,0:T(8,128)} %get-tuple-element.361, s32[]{:T(128)} %get-tuple-element.344, f32[]{:T(128)} %bitcast.60, ...), kind=kOutput, calls=%fused_computation.6.clone.1 | convolution fusion | flops 269254656 | bytes 5408768 | tf_op jit(solution)/shard_map/while/body/eval_jaxpr/dot_general | solution.py:26
  90.5 0.7 multiply_convert_fusion.4
  93.3 3.1 %fusion.52 = f32[256,256]{1,0:T(8,128)S(1)} fusion(f32[256,256]{1,0:T(8,128)S(1)} %get-tuple-element.345, s32[]{:T(128)S(6)} %select_n.33, bf16[4096,256]{1,0:T(8,128)(2,1)S(1)} %bitcast.70, s32[4,64,4096]{2,1,0:T(8,128)} %get-tuple-element.361, s32[]{:T(128)} %get-tuple-element.344, f32[]{:T(128)} %bitcast.60, ...), kind=kOutput, calls=%fused_computation.6.clone.1 | convolution fusion | flops 269254656 | bytes 5408768 | tf_op jit(solution)/shard_map/while/body/eval_jaxpr/dot_general | solution.py:26
  96.4 0.7 copy-done.1
  97.9 21.7 %psum.15 = f32[4,256]{1,0:T(4,128)S(1)} all-reduce(f32[4,256]{1,0:T(4,128)S(1)} %fusion.24), channel_id=1, replica_groups=mesh['ia'=4,'ja'=2,'ka'=4] {'ja','ka'}, use_global_device_ids=true, to_apply=%region_5.6 | all-reduce | flops 1024 | bytes 8192 | tf_op jit(solution)/shard_map/psum | solution.py:50
  119.5 49.9 %all-reduce.2.cloned.1.call-done = f32[256,256]{1,0:T(8,128)} async-done(((f32[256,256]{1,0:T(8,128)}), f32[256,256]{1,0:T(8,128)}) %all-reduce.2.cloned.1.call-update) | async-done | bytes 262160 | tf_op jit(solution)/shard_map/psum | solution.py:71
  169.4 1.0 fusion.33
  170.5 34.4 %while.21 = (s32[]{:T(128)}, f32[256,256]{1,0:T(8,128)S(1)}, s32[4]{0:T(128)S(1)}, s32[4,64,4096]{2,1,0:T(8,128)}, bf16[256,256]{1,0:T(8,128)(2,1)S(1)}, /*index...) while((s32[]{:T(128)}, f32[256,256]{1,0:T(8,128)S(1)}, ...), condition=%wide.region_7.8_spmd, body=%wide.region_6.7_spmd.sunk | while | flops 271351808 | bytes 7899463 | solution.py:64
  173.2 0.7 multiply_convert_fusion.5
  176.0 3.1 %fusion.56 = f32[256,256]{1,0:T(8,128)S(1)} fusion(f32[256,256]{1,0:T(8,128)S(1)} %get-tuple-element.387, s32[]{:T(128)S(6)} %select_n.36, bf16[4096,256]{1,0:T(8,128)(2,1)S(1)} %bitcast.71, s32[4,64,4096]{2,1,0:T(8,128)} %get-tuple-element.403, s32[]{:T(128)} %get-tuple-element.386, f32[]{:T(128)} %bitcast.68, ...), kind=kOutput, calls=%fused_computation.20.clone.1 | convolution fusion | flops 269254656 | bytes 5408768 | tf_op jit(solution)/shard_map/while/body/eval_jaxpr/dot_general | solution.py:26
  181.8 0.7 multiply_convert_fusion.5
  184.6 3.1 %fusion.56 = f32[256,256]{1,0:T(8,128)S(1)} fusion(f32[256,256]{1,0:T(8,128)S(1)} %get-tuple-element.387, s32[]{:T(128)S(6)} %select_n.36, bf16[4096,256]{1,0:T(8,128)(2,1)S(1)} %bitcast.71, s32[4,64,4096]{2,1,0:T(8,128)} %get-tuple-element.403, s32[]{:T(128)} %get-tuple-element.386, f32[]{:T(128)} %bitcast.68, ...), kind=kOutput, calls=%fused_computation.20.clone.1 | convolution fusion | flops 269254656 | bytes 5408768 | tf_op jit(solution)/shard_map/while/body/eval_jaxpr/dot_general | solution.py:26
  190.4 0.7 multiply_convert_fusion.5
  193.2 3.1 %fusion.56 = f32[256,256]{1,0:T(8,128)S(1)} fusion(f32[256,256]{1,0:T(8,128)S(1)} %get-tuple-element.387, s32[]{:T(128)S(6)} %select_n.36, bf16[4096,256]{1,0:T(8,128)(2,1)S(1)} %bitcast.71, s32[4,64,4096]{2,1,0:T(8,128)} %get-tuple-element.403, s32[]{:T(128)} %get-tuple-element.386, f32[]{:T(128)} %bitcast.68, ...), kind=kOutput, calls=%fused_computation.20.clone.1 | convolution fusion | flops 269254656 | bytes 5408768 | tf_op jit(solution)/shard_map/while/body/eval_jaxpr/dot_general | solution.py:26
  199.0 0.7 multiply_convert_fusion.5
  201.8 3.1 %fusion.56 = f32[256,256]{1,0:T(8,128)S(1)} fusion(f32[256,256]{1,0:T(8,128)S(1)} %get-tuple-element.387, s32[]{:T(128)S(6)} %select_n.36, bf16[4096,256]{1,0:T(8,128)(2,1)S(1)} %bitcast.71, s32[4,64,4096]{2,1,0:T(8,128)} %get-tuple-element.403, s32[]{:T(128)} %get-tuple-element.386, f32[]{:T(128)} %bitcast.68, ...), kind=kOutput, calls=%fused_computation.20.clone.1 | convolution fusion | flops 269254656 | bytes 5408768 | tf_op jit(solution)/shard_map/while/body/eval_jaxpr/dot_general | solution.py:26
  204.9 0.7 copy-done
  205.6 61.8 %reduce-scatter.2.cloned.1.call-done = f32[32,256]{1,0:T(8,128)} async-done(((f32[256,256]{1,0:T(8,128)}), f32[32,256]{1,0:T(8,128)}) %reduce-scatter.2.cloned.1.call-update) | async-done | bytes 32784 | tf_op jit(solution)/shard_map/reduce_scatter | solution.py:74
  267.4 1.4 dynamic-slice_divide_fusion
  (55 shorter events, 20.7 us)
Async XLA Ops:
  6.5 162.9 %all-reduce.2.cloned.1.call-start = ((), (), s32[]{:S(2)}) async-start(), calls=%async_computation.1 | async-start | bytes 524288 | tf_op jit(solution)/shard_map/psum | solution.py:71
  96.4 0.7 copy-start.1
  97.1 170.3 %reduce-scatter.2.cloned.1.call-start = ((), (), s32[]{:S(2)}) async-start(), calls=%async_computation.2 | async-start | bytes 294912 | tf_op jit(solution)/shard_map/reduce_scatter | solution.py:74
  204.9 0.7 copy-start
Sparse Core Ops, SparseCore 0:
  97.2 72.1 all-reduce.1
  205.7 61.6 reduce-scatter.1
where the time goes:
time: 277 us; the launch traced here: 276 us
  waiting for transfers between devices  112 us (40%)
  blocking collectives  75.3 us (27%)
  matrix products  25.4 us (9%)
  local copies, waits for them, and re-layouts  24 us (9%)
  loops' own time  17.1 us (6%)
  between operations  14.1 us (5%)
  other arithmetic  7.95 us (3%)
    reduce_scatter x1, waiting for transfers between devices, local(): mine = lax.psum_scatter(phi, ('ja', 'ka'), scatter_dimension=0, tiled=True)  61.8 us
    psum x1, waiting for transfers between devices, local(): totals = lax.psum(phi, ('ja', 'ka'))  49.9 us
    all_gather x1, blocking collectives, local(): whole = lax.all_gather(factor_a, ('ja', 'ka'), axis=0, tiled=True)  31.8 us
    dot_general x8, matrix products, add_block(): part = jnp.dot(ratio, panel, preferred_element_type=jnp.float32) * weight  24.7 us
    psum x1, blocking collectives, local(): mass = lax.psum(mass_part, ('ja', 'ka'))  21.7 us
    dynamic_slice x32, local copies, waits for them, and re-layouts, accumulate(): lax.scan(step, empty, (coords[:, 0], coords[:, 1], coords[:, 2], weights,...  21.4 us
    another operation x2, loops' own time, accumulate(): lax.scan(step, empty, (coords[:, 0], coords[:, 1], coords[:, 2], weights,...  17.1 us
    all_gather x1, blocking collectives, local(): rows_b = lax.all_gather(factor_b, 'ka', axis=0, tiled=True)  14.3 us
  transfers between devices with their start and end apart: 2, of which 2 were waited for; matrix products, arithmetic and copies ran while one was open for 0% of the time, Pallas kernels for 0%

commit v1 on v0

--- a/solution.py
+++ b/solution.py
@@ -68,7 +68,7 @@
 
     whole = lax.all_gather(factor_a, ("ja", "ka"), axis=0, tiled=True)
     phi = accumulate(whole.astype(jnp.bfloat16))
-    totals = lax.psum(phi, ("ja", "ka"))
+    totals = lax.psum(lax.psum(phi, "ja"), "ka")
     updated = whole * totals / mass_rows
     phi = accumulate(updated.astype(jnp.bfloat16))
     mine = lax.psum_scatter(phi, ("ja", "ka"), scatter_dimension=0, tiled=True)

time: 277 us -> 267 us (0.964)
  waiting for transfers between devices: 112 us -> 104 us
    psum x1 -> x2, waiting for transfers between devices: 49.9 us -> 41.3 us  [local(): totals = lax.psum(lax.psum(phi, 'ja'), 'ka')]
  transfers between devices with their start and end apart: 2 -> 3, of which waited for: 2 -> 3; matrix products, arithmetic and copies ran while one was open for 0% -> 0% of each run, Pallas kernels for 0% -> 0%
where the time goes in v1:
time: 267 us; the launch traced here: 266 us
  waiting for transfers between devices  104 us (39%)
  blocking collectives  74.2 us (28%)
  matrix products  25.4 us (10%)
  local copies, waits for them, and re-layouts  24 us (9%)
  loops' own time  17.1 us (6%)
  between operations  13.8 us (5%)
  other arithmetic  7.96 us (3%)
    reduce_scatter x1, waiting for transfers between devices, local(): mine = lax.psum_scatter(phi, ('ja', 'ka'), scatter_dimension=0, tiled=True)  62.4 us
    psum x2, waiting for transfers between devices, local(): totals = lax.psum(lax.psum(phi, 'ja'), 'ka')  41.3 us
    all_gather x1, blocking collectives, local(): whole = lax.all_gather(factor_a, ('ja', 'ka'), axis=0, tiled=True)  31.8 us
    dot_general x8, matrix products, add_block(): part = jnp.dot(ratio, panel, preferred_element_type=jnp.float32) * weight  24.8 us
    dynamic_slice x32, local copies, waits for them, and re-layouts, accumulate(): lax.scan(step, empty, (coords[:, 0], coords[:, 1], coords[:, 2], weights,...  21.4 us
    psum x1, blocking collectives, local(): mass = lax.psum(mass_part, ('ja', 'ka'))  20.6 us
    another operation x2, loops' own time, accumulate(): lax.scan(step, empty, (coords[:, 0], coords[:, 1], coords[:, 2], weights,...  17.1 us
    all_gather x1, blocking collectives, local(): rows_b = lax.all_gather(factor_b, 'ka', axis=0, tiled=True)  14.3 us
  transfers between devices with their start and end apart: 3, of which 3 were waited for; matrix products, arithmetic and copies ran while one was open for 0% of the time, Pallas kernels for 0%

profile of v1, /device:TPU:0, one launch (start us, length us, event | category | flops | bytes accessed | tf_op | source)
XLA Modules:
  0.0 266.5 jit_solution(744197925904572931)
XLA Ops:
  6.5 0.8 copy.14
  7.5 7.5 %all_gather.11 = f32[256,256]{0,1:T(8,128)S(1)} all-gather(f32[256,64]{0,1:T(8,128)} %param.15), channel_id=1, replica_groups=mesh['ia'=4,'ja'=2,'ka'=4] {'ia'}, dimensions={1}, use_global_device_ids=true | all-gather | bytes 327680 | tf_op jit(solution)/shard_map/all_gather | solution.py:36
  15.1 14.3 %all_gather.10 = f32[256,256]{1,0:T(8,128)S(1)} all-gather(f32[64,256]{1,0:T(8,128)} %param.14), channel_id=1, replica_groups=mesh['ia'=4,'ja'=2,'ka'=4] {'ka'}, dimensions={0}, use_global_device_ids=true | all-gather | bytes 327680 | tf_op jit(solution)/shard_map/all_gather | solution.py:35
  30.1 31.8 %all_gather.9 = f32[256,256]{1,0:T(8,128)S(1)} all-gather(f32[32,256]{1,0:T(8,128)} %param.13), channel_id=1, replica_groups=mesh['ia'=4,'ja'=2,'ka'=4] {'ja','ka'}, dimensions={0}, use_global_device_ids=true | all-gather | bytes 294912 | tf_op jit(solution)/shard_map/all_gather | solution.py:69
  62.0 34.5 %while.20 = (s32[]{:T(128)}, f32[256,256]{1,0:T(8,128)S(1)}, s32[4]{0:T(128)S(1)}, s32[4,64,4096]{2,1,0:T(8,128)}, bf16[256,256]{1,0:T(8,128)(2,1)S(1)}, /*index...) while((s32[]{:T(128)}, f32[256,256]{1,0:T(8,128)S(1)}, ...), condition=%wide.region_1.0_spmd, body=%wide.region_0.0_spmd.sunk | while | flops 271351808 | bytes 7899463 | solution.py:64
  64.7 0.7 multiply_convert_fusion.4
  67.5 3.1 %fusion.52 = f32[256,256]{1,0:T(8,128)S(1)} fusion(f32[256,256]{1,0:T(8,128)S(1)} %get-tuple-element.345, s32[]{:T(128)S(6)} %select_n.33, bf16[4096,256]{1,0:T(8,128)(2,1)S(1)} %bitcast.70, s32[4,64,4096]{2,1,0:T(8,128)} %get-tuple-element.361, s32[]{:T(128)} %get-tuple-element.344, f32[]{:T(128)} %bitcast.60, ...), kind=kOutput, calls=%fused_computation.6.clone.1 | convolution fusion | flops 269254656 | bytes 5408768 | tf_op jit(solution)/shard_map/while/body/eval_jaxpr/dot_general | solution.py:26
  73.3 0.7 multiply_convert_fusion.4
  76.1 3.1 %fusion.52 = f32[256,256]{1,0:T(8,128)S(1)} fusion(f32[256,256]{1,0:T(8,128)S(1)} %get-tuple-element.345, s32[]{:T(128)S(6)} %select_n.33, bf16[4096,256]{1,0:T(8,128)(2,1)S(1)} %bitcast.70, s32[4,64,4096]{2,1,0:T(8,128)} %get-tuple-element.361, s32[]{:T(128)} %get-tuple-element.344, f32[]{:T(128)} %bitcast.60, ...), kind=kOutput, calls=%fused_computation.6.clone.1 | convolution fusion | flops 269254656 | bytes 5408768 | tf_op jit(solution)/shard_map/while/body/eval_jaxpr/dot_general | solution.py:26
  82.0 0.7 multiply_convert_fusion.4
  84.7 3.1 %fusion.52 = f32[256,256]{1,0:T(8,128)S(1)} fusion(f32[256,256]{1,0:T(8,128)S(1)} %get-tuple-element.345, s32[]{:T(128)S(6)} %select_n.33, bf16[4096,256]{1,0:T(8,128)(2,1)S(1)} %bitcast.70, s32[4,64,4096]{2,1,0:T(8,128)} %get-tuple-element.361, s32[]{:T(128)} %get-tuple-element.344, f32[]{:T(128)} %bitcast.60, ...), kind=kOutput, calls=%fused_computation.6.clone.1 | convolution fusion | flops 269254656 | bytes 5408768 | tf_op jit(solution)/shard_map/while/body/eval_jaxpr/dot_general | solution.py:26
  90.6 0.7 multiply_convert_fusion.4
  92.6 0.7 dynamic_slice.110
  93.3 3.1 %fusion.52 = f32[256,256]{1,0:T(8,128)S(1)} fusion(f32[256,256]{1,0:T(8,128)S(1)} %get-tuple-element.345, s32[]{:T(128)S(6)} %select_n.33, bf16[4096,256]{1,0:T(8,128)(2,1)S(1)} %bitcast.70, s32[4,64,4096]{2,1,0:T(8,128)} %get-tuple-element.361, s32[]{:T(128)} %get-tuple-element.344, f32[]{:T(128)} %bitcast.60, ...), kind=kOutput, calls=%fused_computation.6.clone.1 | convolution fusion | flops 269254656 | bytes 5408768 | tf_op jit(solution)/shard_map/while/body/eval_jaxpr/dot_general | solution.py:26
  96.4 0.7 copy-done.1
  97.4 24.3 %all-reduce.3.cloned.1.call-done = f32[256,256]{1,0:T(8,128)} async-done(((f32[256,256]{1,0:T(8,128)}), f32[256,256]{1,0:T(8,128)}) %all-reduce.3.cloned.1.call-update) | async-done | bytes 262160 | tf_op jit(solution)/shard_map/psum | solution.py:71
  122.2 20.6 %psum.23 = f32[4,256]{1,0:T(4,128)S(1)} all-reduce(f32[4,256]{1,0:T(4,128)S(1)} %fusion.24), channel_id=1, replica_groups=mesh['ia'=4,'ja'=2,'ka'=4] {'ja','ka'}, use_global_device_ids=true, to_apply=%region_6.7 | all-reduce | flops 1024 | bytes 8192 | tf_op jit(solution)/shard_map/psum | solution.py:50
  142.8 17.1 %all-reduce.5.cloned.1.call-done = f32[256,256]{1,0:T(8,128)} async-done(((f32[256,256]{1,0:T(8,128)}), f32[256,256]{1,0:T(8,128)}) %all-reduce.5.cloned.1.call-update) | async-done | bytes 262160 | tf_op jit(solution)/shard_map/psum | solution.py:71
  159.9 1.0 fusion.33
  160.9 34.4 %while.21 = (s32[]{:T(128)}, f32[256,256]{1,0:T(8,128)S(1)}, s32[4]{0:T(128)S(1)}, s32[4,64,4096]{2,1,0:T(8,128)}, bf16[256,256]{1,0:T(8,128)(2,1)S(1)}, /*index...) while((s32[]{:T(128)}, f32[256,256]{1,0:T(8,128)S(1)}, ...), condition=%wide.region_8.9_spmd, body=%wide.region_7.8_spmd.sunk | while | flops 271351808 | bytes 7899463 | solution.py:64
  162.3 0.7 dynamic_slice.117
  163.7 0.7 multiply_convert_fusion.5
  166.4 3.1 %fusion.56 = f32[256,256]{1,0:T(8,128)S(1)} fusion(f32[256,256]{1,0:T(8,128)S(1)} %get-tuple-element.387, s32[]{:T(128)S(6)} %select_n.36, bf16[4096,256]{1,0:T(8,128)(2,1)S(1)} %bitcast.71, s32[4,64,4096]{2,1,0:T(8,128)} %get-tuple-element.403, s32[]{:T(128)} %get-tuple-element.386, f32[]{:T(128)} %bitcast.68, ...), kind=kOutput, calls=%fused_computation.20.clone.1 | convolution fusion | flops 269254656 | bytes 5408768 | tf_op jit(solution)/shard_map/while/body/eval_jaxpr/dot_general | solution.py:26
  172.3 0.7 multiply_convert_fusion.5
  175.0 3.1 %fusion.56 = f32[256,256]{1,0:T(8,128)S(1)} fusion(f32[256,256]{1,0:T(8,128)S(1)} %get-tuple-element.387, s32[]{:T(128)S(6)} %select_n.36, bf16[4096,256]{1,0:T(8,128)(2,1)S(1)} %bitcast.71, s32[4,64,4096]{2,1,0:T(8,128)} %get-tuple-element.403, s32[]{:T(128)} %get-tuple-element.386, f32[]{:T(128)} %bitcast.68, ...), kind=kOutput, calls=%fused_computation.20.clone.1 | convolution fusion | flops 269254656 | bytes 5408768 | tf_op jit(solution)/shard_map/while/body/eval_jaxpr/dot_general | solution.py:26
  180.9 0.7 multiply_convert_fusion.5
  183.6 3.1 %fusion.56 = f32[256,256]{1,0:T(8,128)S(1)} fusion(f32[256,256]{1,0:T(8,128)S(1)} %get-tuple-element.387, s32[]{:T(128)S(6)} %select_n.36, bf16[4096,256]{1,0:T(8,128)(2,1)S(1)} %bitcast.71, s32[4,64,4096]{2,1,0:T(8,128)} %get-tuple-element.403, s32[]{:T(128)} %get-tuple-element.386, f32[]{:T(128)} %bitcast.68, ...), kind=kOutput, calls=%fused_computation.20.clone.1 | convolution fusion | flops 269254656 | bytes 5408768 | tf_op jit(solution)/shard_map/while/body/eval_jaxpr/dot_general | solution.py:26
  189.5 0.7 multiply_convert_fusion.5
  192.2 3.1 %fusion.56 = f32[256,256]{1,0:T(8,128)S(1)} fusion(f32[256,256]{1,0:T(8,128)S(1)} %get-tuple-element.387, s32[]{:T(128)S(6)} %select_n.36, bf16[4096,256]{1,0:T(8,128)(2,1)S(1)} %bitcast.71, s32[4,64,4096]{2,1,0:T(8,128)} %get-tuple-element.403, s32[]{:T(128)} %get-tuple-element.386, f32[]{:T(128)} %bitcast.68, ...), kind=kOutput, calls=%fused_computation.20.clone.1 | convolution fusion | flops 269254656 | bytes 5408768 | tf_op jit(solution)/shard_map/while/body/eval_jaxpr/dot_general | solution.py:26
  195.3 0.7 copy-done
  196.1 62.4 %reduce-scatter.2.cloned.1.call-done = f32[32,256]{1,0:T(8,128)} async-done(((f32[256,256]{1,0:T(8,128)}), f32[32,256]{1,0:T(8,128)}) %reduce-scatter.2.cloned.1.call-update) | async-done | bytes 32784 | tf_op jit(solution)/shard_map/reduce_scatter | solution.py:74
  258.5 1.4 dynamic-slice_divide_fusion
  (58 shorter events, 21.4 us)
Async XLA Ops:
  6.5 115.2 %all-reduce.3.cloned.1.call-start = ((), (), s32[]{:S(2)}) async-start(), calls=%async_computation.1 | async-start | bytes 524288 | tf_op jit(solution)/shard_map/psum | solution.py:71
  96.4 0.7 copy-start.1
  97.1 62.7 %all-reduce.5.cloned.1.call-start = ((), (), s32[]{:S(2)}) async-start(), calls=%async_computation.2 | async-start | bytes 524288 | tf_op jit(solution)/shard_map/psum | solution.py:71
  121.7 136.8 %reduce-scatter.2.cloned.1.call-start = ((), (), s32[]{:S(2)}) async-start(), calls=%async_computation.3 | async-start | bytes 294912 | tf_op jit(solution)/shard_map/reduce_scatter | solution.py:74
  195.3 0.7 copy-start
Sparse Core Ops, SparseCore 0:
  97.3 24.3 all-reduce.2
  124.0 35.7 all-reduce.4
  196.2 62.2 reduce-scatter.1
